TPU v7x, 32 devices: a whole 2x2x4 slice. The times are simulated.
32 devices in a mesh: groups: 2 (over x), chan: 16 (over z, y, core).
Axes of the slice: x: 2, y: 2, z: 4, core: 2. Of those that a mesh axis runs over, the one named last changes fastest.
Arguments:
- spectra: bfloat16 [2, 8, 512, 512], P(None, 'groups', 'chan'), parts along dimension 1, may hold values from -6 to 6
- filter_bank: float32 [2, 8, 65], replicated, may hold values from -0.5 to 0.5
- band_index: int32 [512], replicated, may hold values from 0 to 7
- window_mask: int32 [8, 512], P('groups', 'chan'), parts along dimension 0, may hold values 0 or 1
- owner_order: int32 [8], P('groups'), parts along dimension 0, may hold values from 0 to 15, as said below
- source_offset: int32 [8, 32], P('groups'), parts along dimension 0, may hold values from 0 to 31, each once within a row
Outputs:
- cross: bfloat16 [2, 256, 512, 512], P(None, 'groups', 'chan'), parts along dimension 1
There are 2 independent parts, one for each index of `groups`. A program takes and returns all parts, laid end to end along the dimension named above; an argument that names none is the same for every part. Nothing has to cross between parts.
Inputs may be any that keep to these rules, and one draw needn't show every extreme that they name: `owner_order`: 4 distinct device indices, below 16.
All inputs are finite; a program needn't handle non-finite values. No bound on the sum of `window_mask` on one device may be relied on, other than what follows from the above.
Results may differ from a plain program's by a relative error of at most 0.0057.
Values may be sent and summed in bfloat16 or wider, within the bound.
A program may use at most 192 MiB of HBM per device.

v0:
```python
import functools

import jax
import jax.numpy as jnp
from jax import lax
from jax.experimental import pallas as pl
from jax.experimental.pallas import tpu as pltpu
from jax.sharding import PartitionSpec as P

SMOOTH = 17
water_level = 0.05
bf16 = jnp.bfloat16
f32 = jnp.float32
LANES = 128


def split(x):
    hi = x.astype(bf16)
    return hi, (x - hi.astype(f32)).astype(bf16)


def build_toeplitz(bank_ref, toep):
    _, nbank, ntap = bank_ref.shape
    chans = toep.shape[1] // (2 * nbank)
    for b in range(nbank):
        parts = []
        for p in range(2):
            row = jnp.concatenate(
                [bank_ref[p, b : b + 1, :], jnp.zeros((1, LANES - ntap), f32)], axis=1
            )
            full = jnp.broadcast_to(row, (chans, LANES))
            parts.append(split(pltpu.roll(full, 0, 1, stride=1, stride_axis=0)))
        at = b * 2 * chans
        for part in range(2):
            real, imag = parts[0][part], parts[1][part]
            toep[part, at : at + chans, :LANES] = real
            toep[part, at : at + chans, LANES:] = -imag
            toep[part, at + chans : at + 2 * chans, :LANES] = imag
            toep[part, at + chans : at + 2 * chans, LANES:] = real


def build_window(band):
    bins = band.shape[0]
    rows = lax.broadcasted_iota(jnp.int32, (bins, bins), 0)
    cols = lax.broadcasted_iota(jnp.int32, (bins, bins), 1)
    band[...] = (jnp.abs(rows - cols) <= SMOOTH // 2).astype(f32).astype(bf16)


def filter_whiten(nbank, xs, toep, band, index_ref, mask_ref, filt, power, out_ref):
    wins, chans = mask_ref.shape
    bins = band.shape[0]
    tile = 256
    for w in range(wins):
        for n in range(bins // tile):
            cut = slice(n * tile, (n + 1) * tile)
            x = xs[w, :, cut]
            res = jnp.dot(toep[0], x, preferred_element_type=f32)
            res += jnp.dot(toep[1], x, preferred_element_type=f32)
            index = index_ref[:, cut]
            acc = res[: 2 * chans]
            for b in range(1, nbank):
                acc = jnp.where(index == b, res[2 * chans * b : 2 * chans * (b + 1)], acc)
            real, imag = acc[:chans], acc[chans:]
            rows = slice(w * chans, (w + 1) * chans)
            filt[0, rows, cut] = real
            filt[1, rows, cut] = imag
            hi, lo = split(real * real + imag * imag)
            power[0, rows, cut] = hi
            power[1, rows, cut] = lo
    smooth = jnp.dot(power[0], band[...], preferred_element_type=f32)
    smooth += jnp.dot(power[1], band[...], preferred_element_type=f32)
    scale = lax.rsqrt(smooth * (1.0 / SMOOTH) + water_level)
    eye = lax.broadcasted_iota(jnp.int32, (chans, chans), 0) == lax.broadcasted_iota(
        jnp.int32, (chans, chans), 1
    )
    for w in range(wins):
        row = jnp.broadcast_to(mask_ref[w : w + 1, :].astype(f32), (chans, chans))
        valid = jnp.sum(jnp.where(eye, row, 0.0), axis=1, keepdims=True)
        rows = slice(w * chans, (w + 1) * chans)
        here = scale[rows] * valid
        for p in range(2):
            out_ref[p, w] = (filt[p, rows] * here).astype(bf16)


def whiten_kernel(
    left_ref, own_ref, right_ref, bank_ref, index_ref, mask_ref, out_ref, xs, toep, band, filt, power
):
    wins, chans = mask_ref.shape
    build_toeplitz(bank_ref, toep)
    build_window(band)
    for p in range(2):
        for w in range(wins):
            at = p * LANES
            xs[w, at : at + chans] = left_ref[p, w]
            xs[w, at + chans : at + 2 * chans] = own_ref[p, w]
            xs[w, at + 2 * chans : at + 3 * chans] = right_ref[p, w]
            xs[w, at + 3 * chans : at + LANES] = jnp.zeros((LANES - 3 * chans, xs.shape[2]), bf16)
    filter_whiten(bank_ref.shape[1], xs, toep, band, index_ref, mask_ref, filt, power, out_ref)


def whiten(left, own, right, bank, index, mask):
    _, wins, chans, bins = own.shape
    nbank = bank.shape[1]
    return pl.pallas_call(
        whiten_kernel,
        out_shape=jax.ShapeDtypeStruct(own.shape, bf16),
        in_specs=[pl.BlockSpec(memory_space=pltpu.VMEM)] * 6,
        out_specs=pl.BlockSpec(memory_space=pltpu.VMEM),
        scratch_shapes=[
            pltpu.VMEM((wins, 2 * LANES, bins), bf16),
            pltpu.VMEM((2, nbank * 2 * chans, 2 * LANES), bf16),
            pltpu.VMEM((bins, bins), bf16),
            pltpu.VMEM((2, wins * chans, bins), f32),
            pltpu.VMEM((2, wins * chans, bins), bf16),
        ],
        name="whiten",
    )(left, own, right, bank, index, mask)


def tree_sum(terms):
    while len(terms) > 1:
        terms = [a + b for a, b in zip(terms[::2], terms[1::2])]
    return terms[0]


def cross_kernel(offset_ref, src_ref, loc_ref, out_ref, wide):
    _, wins, chans, bins = loc_ref.shape
    count = out_ref.shape[1]
    r, h = pl.program_id(0), pl.program_id(1)

    @pl.when(h == 0)
    def _():
        for p in range(2):
            for w in range(wins):
                wide[:, p * wins + w, :] = src_ref[0, p, w].astype(f32) * (1.0 / wins)

    for n in range(bins // LANES):
        cut = slice(n * LANES, (n + 1) * LANES)
        loc = [[loc_ref[p, w, :, cut] for w in range(wins)] for p in range(2)]

        def one(j, carry, cut=cut, loc=loc):
            at = offset_ref[r, h * count + j]
            src = [
                [
                    jnp.broadcast_to(
                        wide[at, p * wins + w : p * wins + w + 1, cut], (chans, LANES)
                    ).astype(bf16)
                    for w in range(wins)
                ]
                for p in range(2)
            ]
            real = tree_sum(
                [src[p][w] * loc[p][w] for w in range(wins) for p in range(2)]
            )
            plus = tree_sum([src[0][w] * loc[1][w] for w in range(wins)])
            minus = tree_sum([src[1][w] * loc[0][w] for w in range(wins)])
            out_ref[0, j, :, cut] = real
            out_ref[1, j, :, cut] = plus - minus
            return carry

        lax.fori_loop(0, count, one, 0, unroll=4)


def cross(offset, src, loc, blocks=2):
    rounds, _, wins, chans, bins = src.shape
    per = chans // blocks
    return pl.pallas_call(
        cross_kernel,
        out_shape=jax.ShapeDtypeStruct((2, rounds * chans, chans, bins), bf16),
        grid=(rounds, blocks),
        in_specs=[
            pl.BlockSpec(memory_space=pltpu.SMEM),
            pl.BlockSpec((1, 2, wins, chans, bins), lambda r, h: (r, 0, 0, 0, 0)),
            pl.BlockSpec((2, wins, chans, bins), lambda r, h: (0, 0, 0, 0)),
        ],
        out_specs=pl.BlockSpec((2, per, chans, bins), lambda r, h: (0, r * blocks + h, 0, 0)),
        scratch_shapes=[pltpu.VMEM((chans, 2 * wins, bins), f32)],
        name="cross",
    )(offset, src, loc)


def body(spectra, filter_bank, band_index, window_mask, owner_order, source_offset):
    count = lax.axis_size("chan")
    ends = count - 1
    left = lax.ppermute(spectra, "chan", [(i, i + 1) for i in range(ends)])
    right = lax.ppermute(spectra, "chan", [(i + 1, i) for i in range(ends)])
    whitened = whiten(left, spectra, right, filter_bank, band_index[None, :], window_mask)
    here = (lax.axis_index("chan") == owner_order)[:, None, None, None, None]
    stacked = jnp.where(here, whitened[None], jnp.zeros((), bf16))
    summed = lax.psum(stacked, "chan")
    return cross(source_offset, summed, whitened)


def solution(mesh):
    in_specs = (
        P(None, "groups", "chan", None),
        P(),
        P(),
        P("groups", "chan"),
        P("groups"),
        P("groups", None),
    )
    out_specs = P(None, "groups", "chan", None)
    return jax.shard_map(body, mesh=mesh, in_specs=in_specs, out_specs=out_specs, check_vma=False)
```

profile of v0, /device:TPU:1, one launch (start us, length us, event | category | flops | bytes accessed | tf_op | source)
XLA Modules:
  0.0 136.5 jit_solution(7288308632412099789)
XLA Ops:
  6.5 0.0 all-reduce.2.cloned.1.call-start
  6.5 4.5 %collective-permute-start = (bf16[2,4,32,512]{3,2,1,0:T(8,128)(2,1)}, bf16[2,4,32,512]{3,2,1,0:T(8,128)(2,1)S(1)}, u32[]{:S(2)}, u32[]{:S(2)}) collective-permute-start(bf16[2,4,32,512]{3,2,1,0:T(8,128)(2,1)} %own_ref.1), channel_id=1, source_target_pairs={{0,1},{1,2},{2,3},{3,4},{4,5},{5,6},{6,7},{7,8},{8,9},{9,10},{10,1... | collective-permute-start | bytes 786440 | tf_op jit(solution)/shard_map/ppermute | solution.py:185
  11.1 1.9 %collective-permute-start.1 = (bf16[2,4,32,512]{3,2,1,0:T(8,128)(2,1)}, bf16[2,4,32,512]{3,2,1,0:T(8,128)(2,1)S(1)}, u32[]{:S(2)}, u32[]{:S(2)}) collective-permute-start(bf16[2,4,32,512]{3,2,1,0:T(8,128)(2,1)} %own_ref.1), channel_id=1, source_target_pairs={{1,0},{2,1},{3,2},{4,3},{5,4},{6,5},{7,6},{8,7},{9,8},{10,9},{11,1... | collective-permute-start | bytes 786440 | tf_op jit(solution)/shard_map/ppermute | solution.py:186
  13.0 0.7 broadcast_compare_fusion
  13.7 1.0 collective-permute-done.left_ref
  14.7 0.0 copy-start
  14.7 4.3 %collective-permute-done.1.right_ref = bf16[2,4,32,512]{3,2,1,0:T(8,128)(2,1)S(1)} collective-permute-done((bf16[2,4,32,512]{3,2,1,0:T(8,128)(2,1)}, bf16[2,4,32,512]{3,2,1,0:T(8,128)(2,1)S(1)}, u32[]{:S(2)}, u32[]{:S(2)}) %collective-permute-start.1) | collective-permute-done | bytes 262176 | tf_op jit(solution)/shard_map/ppermute | solution.py:186
  19.0 0.0 copy-start.1
  19.0 0.0 copy-done
  19.0 0.7 copy-done.1
  19.7 3.4 %whiten.1.loc_ref = bf16[2,4,32,512]{3,2,1,0:T(8,128)(2,1)} custom-call(bf16[2,4,32,512]{3,2,1,0:T(8,128)(2,1)} %copy-done, bf16[2,4,32,512]{3,2,1,0:T(8,128)(2,1)} %own_ref.1, bf16[2,4,32,512]{3,2,1,0:T(8,128)(2,1)} %copy-done.1, f32[2,8,65]{2,1,0:T(8,128)} %bank_ref.1, s32[1,512]{1,0:T(1,128)} %bitcast.1, s32[4,32]{1,0:T(4,128)} %mask_ref.1), custom_call_target="tpu_custom_call" | custom-call | tf_op jit(solution)/shard_map/whiten/pallas_call | solution.py:104
  23.1 2.1 %broadcast_select_fusion = bf16[4,2,4,32,512]{4,3,2,1,0:T(8,128)(2,1)} fusion(pred[4]{0:T(512)(128)(4,1)S(1)} %broadcast_compare_fusion, bf16[2,4,32,512]{3,2,1,0:T(8,128)(2,1)} %whiten.1.loc_ref), kind=kLoop, calls=%fused_computation | loop fusion | flops 524288 | bytes 1310724 | tf_op jit(solution)/shard_map/jit(_where)/select_n | solution.py:189
  25.1 0.0 all-reduce.2.cloned.1.call-update
  25.2 93.8 %all-reduce.2.cloned.1.call-done.src_ref = bf16[4,2,4,32,512]{4,3,2,1,0:T(8,128)(2,1)} async-done(((bf16[4,2,4,32,512]{4,3,2,1,0:T(8,128)(2,1)}), bf16[4,2,4,32,512]{4,3,2,1,0:T(8,128)(2,1)}) %all-reduce.2.cloned.1.call-update) | async-done | bytes 1048592 | tf_op jit(solution)/shard_map/psum | solution.py:190
  118.9 10.7 %cross.1 = bf16[2,128,32,512]{3,2,1,0:T(8,128)(2,1)} custom-call(s32[4,32]{1,0:T(4,128)} %offset_ref.1, bf16[4,2,4,32,512]{4,3,2,1,0:T(8,128)(2,1)} %all-reduce.2.cloned.1.call-done.src_ref, bf16[2,4,32,512]{3,2,1,0:T(8,128)(2,1)} %whiten.1.loc_ref), custom_call_target="tpu_custom_call" | custom-call | tf_op jit(solution)/shard_map/cross/pallas_call | solution.py:167
Async XLA Ops:
  6.5 112.4 %all-reduce.2.cloned.1.call-start = ((), (), s32[]{:S(2)}) async-start(), calls=%async_computation | async-start | bytes 2097152 | tf_op jit(solution)/shard_map/psum | solution.py:190
  6.5 8.1 %collective-permute-start = (bf16[2,4,32,512]{3,2,1,0:T(8,128)(2,1)}, bf16[2,4,32,512]{3,2,1,0:T(8,128)(2,1)S(1)}, u32[]{:S(2)}, u32[]{:S(2)}) collective-permute-start(bf16[2,4,32,512]{3,2,1,0:T(8,128)(2,1)} %own_ref.1), channel_id=1, source_target_pairs={{0,1},{1,2},{2,3},{3,4},{4,5},{5,6},{6,7},{7,8},{8,9},{9,10},{10,1... | collective-permute-start | bytes 786440 | tf_op jit(solution)/shard_map/ppermute | solution.py:185
  11.1 7.9 %collective-permute-start.1 = (bf16[2,4,32,512]{3,2,1,0:T(8,128)(2,1)}, bf16[2,4,32,512]{3,2,1,0:T(8,128)(2,1)S(1)}, u32[]{:S(2)}, u32[]{:S(2)}) collective-permute-start(bf16[2,4,32,512]{3,2,1,0:T(8,128)(2,1)} %own_ref.1), channel_id=1, source_target_pairs={{1,0},{2,1},{3,2},{4,3},{5,4},{6,5},{7,6},{8,7},{9,8},{10,9},{11,1... | collective-permute-start | bytes 786440 | tf_op jit(solution)/shard_map/ppermute | solution.py:186
  14.7 4.3 %copy-start = (bf16[2,4,32,512]{3,2,1,0:T(8,128)(2,1)}, bf16[2,4,32,512]{3,2,1,0:T(8,128)(2,1)S(1)}, u32[]{:S(2)}) copy-start(bf16[2,4,32,512]{3,2,1,0:T(8,128)(2,1)S(1)} %collective-permute-done.left_ref) | copy-start | bytes 786436
  19.0 0.7 copy-start.1
Sparse Core Ops, SparseCore 0:
  25.3 93.6 all-reduce.1
where the time goes:
time: 138 us; the launch traced here: 136 us
  waiting for transfers between devices  99.1 us (72%)
  Pallas kernels  14.1 us (10%)
  between operations  13.4 us (10%)
  starting transfers between devices  6.44 us (5%)
  other arithmetic  2.72 us (2%)
    psum x1, waiting for transfers between devices, body(): summed = lax.psum(stacked, 'chan')  93.8 us
    pallas_call x1, Pallas kernels, cross(): pl.pallas_call(cross_kernel, out_shape=jax.ShapeDtypeStruct((2, rounds *...  10.7 us
    ppermute x1, starting transfers between devices, body(): left = lax.ppermute(spectra, 'chan', [(i, i + 1) for i in range(ends)])  4.52 us
    ppermute x1, waiting for transfers between devices, body(): right = lax.ppermute(spectra, 'chan', [(i + 1, i) for i in range(ends)])  4.29 us
    pallas_call x1, Pallas kernels, whiten(): pl.pallas_call(whiten_kernel, out_shape=jax.ShapeDtypeStruct(own.shape, b...  3.43 us
  transfers between devices with their start and end apart: 3, of which 3 were waited for; matrix products, arithmetic and copies ran while one was open for 0% of the time, Pallas kernels for 0%

commit v1 on v0

--- a/solution.py
+++ b/solution.py
@@ -46,75 +46,323 @@
     band[...] = (jnp.abs(rows - cols) <= SMOOTH // 2).astype(f32).astype(bf16)
 
 
-def filter_whiten(nbank, xs, toep, band, index_ref, mask_ref, filt, power, out_ref):
-    wins, chans = mask_ref.shape
-    bins = band.shape[0]
+def filter_window(nbank, w, x, toep, index_ref, filt, power):
+    bins = filt.shape[2]
+    chans = toep.shape[1] // (2 * nbank)
     tile = 256
-    for w in range(wins):
-        for n in range(bins // tile):
-            cut = slice(n * tile, (n + 1) * tile)
-            x = xs[w, :, cut]
-            res = jnp.dot(toep[0], x, preferred_element_type=f32)
-            res += jnp.dot(toep[1], x, preferred_element_type=f32)
-            index = index_ref[:, cut]
-            acc = res[: 2 * chans]
-            for b in range(1, nbank):
-                acc = jnp.where(index == b, res[2 * chans * b : 2 * chans * (b + 1)], acc)
-            real, imag = acc[:chans], acc[chans:]
-            rows = slice(w * chans, (w + 1) * chans)
-            filt[0, rows, cut] = real
-            filt[1, rows, cut] = imag
-            hi, lo = split(real * real + imag * imag)
-            power[0, rows, cut] = hi
-            power[1, rows, cut] = lo
-    smooth = jnp.dot(power[0], band[...], preferred_element_type=f32)
-    smooth += jnp.dot(power[1], band[...], preferred_element_type=f32)
+    rows = slice(w * chans, (w + 1) * chans)
+    for n in range(bins // tile):
+        cut = slice(n * tile, (n + 1) * tile)
+        here = x(cut)
+        res = jnp.dot(toep[0], here, preferred_element_type=f32)
+        res += jnp.dot(toep[1], here, preferred_element_type=f32)
+        index = index_ref[:, cut]
+        acc = res[: 2 * chans]
+        for b in range(1, nbank):
+            acc = jnp.where(index == b, res[2 * chans * b : 2 * chans * (b + 1)], acc)
+        real, imag = acc[:chans], acc[chans:]
+        filt[0, rows, cut] = real
+        filt[1, rows, cut] = imag
+        hi, lo = split(real * real + imag * imag)
+        power[0, rows, cut] = hi
+        power[1, rows, cut] = lo
+
+
+def whiten_window(w, band, mask_ref, filt, power):
+    chans = mask_ref.shape[1]
+    rows = slice(w * chans, (w + 1) * chans)
+    smooth = jnp.dot(power[0, rows], band[...], preferred_element_type=f32)
+    smooth += jnp.dot(power[1, rows], band[...], preferred_element_type=f32)
     scale = lax.rsqrt(smooth * (1.0 / SMOOTH) + water_level)
     eye = lax.broadcasted_iota(jnp.int32, (chans, chans), 0) == lax.broadcasted_iota(
         jnp.int32, (chans, chans), 1
     )
-    for w in range(wins):
-        row = jnp.broadcast_to(mask_ref[w : w + 1, :].astype(f32), (chans, chans))
-        valid = jnp.sum(jnp.where(eye, row, 0.0), axis=1, keepdims=True)
-        rows = slice(w * chans, (w + 1) * chans)
-        here = scale[rows] * valid
-        for p in range(2):
-            out_ref[p, w] = (filt[p, rows] * here).astype(bf16)
-
-
-def whiten_kernel(
-    left_ref, own_ref, right_ref, bank_ref, index_ref, mask_ref, out_ref, xs, toep, band, filt, power
+    row = jnp.broadcast_to(mask_ref[w : w + 1, :].astype(f32), (chans, chans))
+    valid = jnp.sum(jnp.where(eye, row, 0.0), axis=1, keepdims=True)
+    scale = scale * valid
+    return [(filt[p, rows] * scale).astype(bf16) for p in range(2)]
+
+
+class Line:
+    def __init__(self, pos, length, device_of, lead, refs):
+        self.pos, self.length, self.device_of, self.lead = pos, length, device_of, lead
+        self.own, self.out_r, self.out_l, self.in_r, self.in_l, self.sems = refs
+        self.count = self.own.shape[0]
+
+    def clear(self):
+        @pl.when(self.pos == 0)
+        def _():
+            self.in_r[...] = jnp.zeros_like(self.in_r)
+
+        @pl.when(self.pos == self.length - 1)
+        def _():
+            self.in_l[...] = jnp.zeros_like(self.in_l)
+
+    def copy(self, way, k):
+        out, into = (self.out_r, self.in_r) if way == 0 else (self.out_l, self.in_l)
+        other = self.pos + 1 if way == 0 else self.pos - 1
+        return pltpu.make_async_remote_copy(
+            src_ref=out.at[k],
+            dst_ref=into.at[k],
+            send_sem=self.sems.at[way, 0, k],
+            recv_sem=self.sems.at[way, 1, k],
+            device_id={"chan": self.device_of(other)},
+            device_id_type=pl.DeviceIdType.MESH,
+        )
+
+    def tick(self, t):
+        for way in range(2):
+            behind = self.pos if way == 0 else self.length - 1 - self.pos
+            out, into = (self.out_r, self.in_r) if way == 0 else (self.out_l, self.in_l)
+            k = t - self.lead - behind
+            inside = jnp.logical_and(k >= 0, k < self.count)
+
+            @pl.when(jnp.logical_and(inside, behind > 0))
+            def _(way=way, k=k):
+                self.copy(way, k).wait_recv()
+
+            @pl.when(jnp.logical_and(inside, behind < self.length - 1))
+            def _(way=way, k=k, out=out, into=into):
+                out[k] = self.own[k] + into[k]
+                self.copy(way, k).start()
+
+    def result(self, k):
+        return self.own[k] + self.in_r[k] + self.in_l[k]
+
+    def drain(self):
+        for way in range(2):
+            behind = self.pos if way == 0 else self.length - 1 - self.pos
+
+            @pl.when(behind < self.length - 1)
+            def _(way=way):
+                @pl.loop(0, self.count)
+                def _(k):
+                    self.copy(way, k).wait_send()
+
+
+def front_kernel(
+    rows,
+    cols,
+    owner_ref,
+    own_ref,
+    bank_ref,
+    index_ref,
+    mask_ref,
+    out_ref,
+    src_ref,
+    halo,
+    toep,
+    band,
+    filt,
+    power,
+    mine,
+    paired,
+    col_buf,
+    row_buf,
+    done,
+    other,
+    halo_sems,
+    pair_sems,
+    col_sems,
+    row_sems,
+    done_sems,
 ):
     wins, chans = mask_ref.shape
+    bins = own_ref.shape[3]
+    half = wins // 2
+    me = lax.axis_index("chan")
+    size = rows * cols * 2
+    core = me % 2
+    col = (me // 2) % cols
+    row = me // (2 * cols)
+    partner = me + 1 - 2 * core
+    mesh_id = pl.DeviceIdType.MESH
+
+    barrier = pltpu.get_barrier_semaphore()
+    partners = [
+        (me > 0, me - 1),
+        (me < size - 1, me + 1),
+        (me >= 0, partner),
+        (col > 0, me - 2),
+        (col < cols - 1, me + 2),
+        (row > 0, me - 2 * cols),
+        (row < rows - 1, me + 2 * cols),
+    ]
+    expected = jnp.int32(0)
+    for there, who in partners:
+        expected += there.astype(jnp.int32)
+
+        @pl.when(there)
+        def _(who=who):
+            pl.semaphore_signal(barrier, inc=1, device_id={"chan": who}, device_id_type=mesh_id)
+
+    pl.semaphore_wait(barrier, expected)
+
+    def halo_copy(way, w):
+        return pltpu.make_async_remote_copy(
+            src_ref=own_ref.at[:, w],
+            dst_ref=halo.at[way, :, w],
+            send_sem=halo_sems.at[way, 0, w],
+            recv_sem=halo_sems.at[way, 1, w],
+            device_id={"chan": me + 1 - 2 * way},
+            device_id_type=mesh_id,
+        )
+
+    sends = (me < size - 1, me > 0)
+    for w in range(wins):
+        for way in range(2):
+
+            @pl.when(sends[way])
+            def _(way=way, w=w):
+                halo_copy(way, w).start()
+
+    for way in range(2):
+
+        @pl.when(jnp.logical_not(sends[1 - way]))
+        def _(way=way):
+            halo[way] = jnp.zeros_like(halo[way])
+
+    line_col = Line(col, cols, lambda i: (row * cols + i) * 2 + core, 0, (*col_buf, col_sems))
+    line_row = Line(row, rows, lambda i: (i * cols + col) * 2 + core, cols - 1, (*row_buf, row_sems))
+    line_col.clear()
+    line_row.clear()
     build_toeplitz(bank_ref, toep)
     build_window(band)
-    for p in range(2):
+
+    blank = jnp.zeros((LANES - 3 * chans, bins), bf16)
+    for w in range(wins):
+        for way in range(2):
+
+            @pl.when(sends[1 - way])
+            def _(way=way, w=w):
+                halo_copy(way, w).wait_recv()
+
+        def x(cut, w=w):
+            parts = []
+            for p in range(2):
+                parts += [halo[0, p, w, :, cut], own_ref[p, w, :, cut], halo[1, p, w, :, cut]]
+                parts += [blank[:, cut]]
+            return jnp.concatenate(parts, axis=0)
+
+        filter_window(bank_ref.shape[1], w, x, toep, index_ref, filt, power)
+    for w in range(wins):
+        white = whiten_window(w, band, mask_ref, filt, power)
+        for p in range(2):
+            out_ref[p, w] = white[p]
+            mine[w, p] = white[p]
+
+    pair = pltpu.make_async_remote_copy(
+        src_ref=mine.at[pl.ds((1 - core) * half, half)],
+        dst_ref=paired,
+        send_sem=pair_sems.at[0],
+        recv_sem=pair_sems.at[1],
+        device_id={"chan": partner},
+        device_id_type=mesh_id,
+    )
+    pair.start()
+    pair.wait_recv()
+
+    count = line_col.count
+    own = col_buf[0]
+
+    @pl.loop(0, count)
+    def _(k):
+        r, w = k // half, k % half
+        first = (owner_ref[r] == me).astype(f32).astype(bf16)
+        second = (owner_ref[r] == partner).astype(f32).astype(bf16)
+        own[k] = mine[core * half + w] * first + paired[w] * second
+
+    def done_copy(k):
+        return pltpu.make_async_remote_copy(
+            src_ref=done.at[k],
+            dst_ref=other.at[k],
+            send_sem=done_sems.at[0, k],
+            recv_sem=done_sems.at[1, k],
+            device_id={"chan": partner},
+            device_id_type=mesh_id,
+        )
+
+    @pl.loop(0, count + cols + rows - 2)
+    def _(t):
+        k = t - (cols - 1)
+        line_col.tick(t)
+
+        @pl.when(jnp.logical_and(k >= 0, k < count))
+        def _():
+            line_row.own[k] = line_col.result(k)
+
+        line_row.tick(t)
+        last = t - (cols - 1) - (rows - 1)
+
+        @pl.when(jnp.logical_and(last >= 0, last < count))
+        def _():
+            total = line_row.result(last)
+            done[last] = total
+            done_copy(last).start()
+            for p in range(2):
+                src_ref[last // half, p, core * half + last % half] = total[p]
+
+    @pl.loop(0, count)
+    def _(k):
+        done_copy(k).wait_recv()
+        for p in range(2):
+            src_ref[k // half, p, (1 - core) * half + k % half] = other[k, p]
+
+    for way in range(2):
         for w in range(wins):
-            at = p * LANES
-            xs[w, at : at + chans] = left_ref[p, w]
-            xs[w, at + chans : at + 2 * chans] = own_ref[p, w]
-            xs[w, at + 2 * chans : at + 3 * chans] = right_ref[p, w]
-            xs[w, at + 3 * chans : at + LANES] = jnp.zeros((LANES - 3 * chans, xs.shape[2]), bf16)
-    filter_whiten(bank_ref.shape[1], xs, toep, band, index_ref, mask_ref, filt, power, out_ref)
-
-
-def whiten(left, own, right, bank, index, mask):
+
+            @pl.when(sends[way])
+            def _(way=way, w=w):
+                halo_copy(way, w).wait_send()
+
+    pair.wait_send()
+    line_col.drain()
+    line_row.drain()
+
+    @pl.loop(0, count)
+    def _(k):
+        done_copy(k).wait_send()
+
+
+def front(grid, owner, own, bank, index, mask):
     _, wins, chans, bins = own.shape
     nbank = bank.shape[1]
+    rounds = owner.shape[0]
+    rows, cols = grid
+    half = wins // 2
+    count = rounds * half
+    vmem = pl.BlockSpec(memory_space=pltpu.VMEM)
+    chunk = (2, chans, bins)
+    chunks = pltpu.VMEM((count, *chunk), bf16)
     return pl.pallas_call(
-        whiten_kernel,
-        out_shape=jax.ShapeDtypeStruct(own.shape, bf16),
-        in_specs=[pl.BlockSpec(memory_space=pltpu.VMEM)] * 6,
-        out_specs=pl.BlockSpec(memory_space=pltpu.VMEM),
+        functools.partial(front_kernel, rows, cols),
+        out_shape=[
+            jax.ShapeDtypeStruct(own.shape, bf16),
+            jax.ShapeDtypeStruct((rounds, *own.shape), bf16),
+        ],
+        in_specs=[pl.BlockSpec(memory_space=pltpu.SMEM)] + [vmem] * 4,
+        out_specs=[vmem] * 2,
         scratch_shapes=[
-            pltpu.VMEM((wins, 2 * LANES, bins), bf16),
+            pltpu.VMEM((2, *own.shape), bf16),
             pltpu.VMEM((2, nbank * 2 * chans, 2 * LANES), bf16),
             pltpu.VMEM((bins, bins), bf16),
             pltpu.VMEM((2, wins * chans, bins), f32),
             pltpu.VMEM((2, wins * chans, bins), bf16),
+            pltpu.VMEM((wins, *chunk), bf16),
+            pltpu.VMEM((half, *chunk), bf16),
+            [chunks] * 5,
+            [chunks] * 5,
+            chunks,
+            chunks,
+            pltpu.SemaphoreType.DMA((2, 2, wins)),
+            pltpu.SemaphoreType.DMA((2,)),
+            pltpu.SemaphoreType.DMA((2, 2, count)),
+            pltpu.SemaphoreType.DMA((2, 2, count)),
+            pltpu.SemaphoreType.DMA((2, count)),
         ],
-        name="whiten",
-    )(left, own, right, bank, index, mask)
+        compiler_params=pltpu.CompilerParams(collective_id=0, has_side_effects=True),
+        name="front",
+    )(owner, own, bank, index, mask)
 
 
 def tree_sum(terms):
@@ -179,16 +427,20 @@
     )(offset, src, loc)
 
 
+def chip_grid(size):
+    chips = size // 2
+    cols = 1
+    while cols * cols * 4 <= chips:
+        cols *= 2
+    return chips // cols, cols
+
+
 def body(spectra, filter_bank, band_index, window_mask, owner_order, source_offset):
-    count = lax.axis_size("chan")
-    ends = count - 1
-    left = lax.ppermute(spectra, "chan", [(i, i + 1) for i in range(ends)])
-    right = lax.ppermute(spectra, "chan", [(i + 1, i) for i in range(ends)])
-    whitened = whiten(left, spectra, right, filter_bank, band_index[None, :], window_mask)
-    here = (lax.axis_index("chan") == owner_order)[:, None, None, None, None]
-    stacked = jnp.where(here, whitened[None], jnp.zeros((), bf16))
-    summed = lax.psum(stacked, "chan")
-    return cross(source_offset, summed, whitened)
+    grid = chip_grid(lax.axis_size("chan"))
+    whitened, sources = front(
+        grid, owner_order, spectra, filter_bank, band_index[None, :], window_mask
+    )
+    return cross(source_offset, sources, whitened)
 
 
 def solution(mesh):

time: 138 us -> 63.4 us (0.46)
  waiting for transfers between devices: 99.1 us -> 0 us
  Pallas kernels: 14.1 us -> 62.9 us
  between operations: 13.4 us -> 0.01 us
  starting transfers between devices: 6.44 us -> 0 us
  other arithmetic: 2.72 us -> 0 us
    psum x1 -> x0, waiting for transfers between devices: 93.8 us -> none  [body(): summed = lax.psum(stacked, 'chan')]
    pallas_call x1, Pallas kernels: 3.43 us -> 52.1 us  [front(): pl.pallas_call(functools.partial(front_kernel, rows, cols), out_shape=[ja...]
    ppermute x2 -> x0, starting transfers between devices: 6.44 us -> none  [the longest x1 4.52 us: body(): left = lax.ppermute(spectra, 'chan', [(i, i + 1) for i in range(ends)])]
    ppermute x2 -> x0, waiting for transfers between devices: 5.3 us -> none  [the longest x1 4.29 us: body(): right = lax.ppermute(spectra, 'chan', [(i + 1, i) for i in range(ends)])]
    select_n x1 -> x0, other arithmetic: 2.06 us -> none  [body(): stacked = jnp.where(here, whitened[None], jnp.zeros((), bf16))]
  transfers between devices with their start and end apart: 3 -> 0, of which waited for: 3 -> 0; matrix products, arithmetic and copies ran while one was open for 0% -> 0% of each run, Pallas kernels for 0% -> 0%
where the time goes in v1:
time: 63.4 us; the launch traced here: 62.9 us
  Pallas kernels  62.9 us (99%)
    pallas_call x1, Pallas kernels, front(): pl.pallas_call(functools.partial(front_kernel, rows, cols), out_shape=[ja...  52.1 us
    pallas_call x1, Pallas kernels, cross(): pl.pallas_call(cross_kernel, out_shape=jax.ShapeDtypeStruct((2, rounds *...  10.7 us

profile of v1, /device:TPU:1, one launch (start us, length us, event | category | flops | bytes accessed | tf_op | source)
XLA Modules:
  0.0 62.9 jit_solution(17234352860947110482)
XLA Ops:
  0.0 52.1 %front.1 = (bf16[2,4,32,512]{3,2,1,0:T(8,128)(2,1)}, bf16[4,2,4,32,512]{4,3,2,1,0:T(8,128)(2,1)}) custom-call(s32[4]{0:T(128)} %owner_ref.1, bf16[2,4,32,512]{3,2,1,0:T(8,128)(2,1)} %own_ref.1, f32[2,8,65]{2,1,0:T(8,128)} %bank_ref.1, s32[1,512]{1,0:T(1,128)} %bitcast.1, s32[4,32]{1,0:T(4,128)} %mask_ref.1), custom_call_target="tpu_custom_call" | custom-call | tf_op jit(solution)/shard_map/front/pallas_call | solution.py:337
  52.1 10.7 %cross.1 = bf16[2,128,32,512]{3,2,1,0:T(8,128)(2,1)} custom-call(s32[4,32]{1,0:T(4,128)} %offset_ref.1, bf16[4,2,4,32,512]{4,3,2,1,0:T(8,128)(2,1)} %get-tuple-element.7.src_ref, bf16[2,4,32,512]{3,2,1,0:T(8,128)(2,1)} %get-tuple-element.8.loc_ref), custom_call_target="tpu_custom_call" | custom-call | tf_op jit(solution)/shard_map/cross/pallas_call | solution.py:415

commit v2 on v1

--- a/solution.py
+++ b/solution.py
@@ -12,6 +12,7 @@
 bf16 = jnp.bfloat16
 f32 = jnp.float32
 LANES = 128
+LAG = 4
 
 
 def split(x):
@@ -84,8 +85,8 @@
 
 
 class Line:
-    def __init__(self, pos, length, device_of, lead, refs):
-        self.pos, self.length, self.device_of, self.lead = pos, length, device_of, lead
+    def __init__(self, pos, length, device_of, lag, refs):
+        self.pos, self.length, self.device_of, self.lag = pos, length, device_of, lag
         self.own, self.out_r, self.out_l, self.in_r, self.in_l, self.sems = refs
         self.count = self.own.shape[0]
 
@@ -114,7 +115,7 @@
         for way in range(2):
             behind = self.pos if way == 0 else self.length - 1 - self.pos
             out, into = (self.out_r, self.in_r) if way == 0 else (self.out_l, self.in_l)
-            k = t - self.lead - behind
+            k = t - self.lag * behind
             inside = jnp.logical_and(k >= 0, k < self.count)
 
             @pl.when(jnp.logical_and(inside, behind > 0))
@@ -156,24 +157,24 @@
     filt,
     power,
     mine,
-    paired,
-    col_buf,
+    beside,
     row_buf,
     done,
     other,
     halo_sems,
-    pair_sems,
-    col_sems,
+    beside_sems,
     row_sems,
     done_sems,
 ):
     wins, chans = mask_ref.shape
     bins = own_ref.shape[3]
     half = wins // 2
+    rounds = src_ref.shape[0]
     me = lax.axis_index("chan")
     size = rows * cols * 2
     core = me % 2
-    col = (me // 2) % cols
+    place = me % (2 * cols)
+    base = me - place
     row = me // (2 * cols)
     partner = me + 1 - 2 * core
     mesh_id = pl.DeviceIdType.MESH
@@ -182,12 +183,9 @@
     partners = [
         (me > 0, me - 1),
         (me < size - 1, me + 1),
-        (me >= 0, partner),
-        (col > 0, me - 2),
-        (col < cols - 1, me + 2),
         (row > 0, me - 2 * cols),
         (row < rows - 1, me + 2 * cols),
-    ]
+    ] + [(place != j, base + j) for j in range(2 * cols)]
     expected = jnp.int32(0)
     for there, who in partners:
         expected += there.astype(jnp.int32)
@@ -208,8 +206,9 @@
             device_id_type=mesh_id,
         )
 
+    order = [c * half + w for w in range(half) for c in range(2)]
     sends = (me < size - 1, me > 0)
-    for w in range(wins):
+    for w in order:
         for way in range(2):
 
             @pl.when(sends[way])
@@ -222,15 +221,23 @@
         def _(way=way):
             halo[way] = jnp.zeros_like(halo[way])
 
-    line_col = Line(col, cols, lambda i: (row * cols + i) * 2 + core, 0, (*col_buf, col_sems))
-    line_row = Line(row, rows, lambda i: (i * cols + col) * 2 + core, cols - 1, (*row_buf, row_sems))
-    line_col.clear()
-    line_row.clear()
+    line = Line(row, rows, lambda i: i * 2 * cols + place, LAG, (*row_buf, row_sems))
+    line.clear()
     build_toeplitz(bank_ref, toep)
     build_window(band)
 
+    def beside_copy(sender, j, w):
+        return pltpu.make_async_remote_copy(
+            src_ref=mine.at[w],
+            dst_ref=beside.at[sender, w % half],
+            send_sem=beside_sems.at[0, j, w % half],
+            recv_sem=beside_sems.at[1, sender, w % half],
+            device_id={"chan": base + j},
+            device_id_type=mesh_id,
+        )
+
     blank = jnp.zeros((LANES - 3 * chans, bins), bf16)
-    for w in range(wins):
+    for w in order:
         for way in range(2):
 
             @pl.when(sends[1 - way])
@@ -245,32 +252,21 @@
             return jnp.concatenate(parts, axis=0)
 
         filter_window(bank_ref.shape[1], w, x, toep, index_ref, filt, power)
-    for w in range(wins):
         white = whiten_window(w, band, mask_ref, filt, power)
         for p in range(2):
             out_ref[p, w] = white[p]
             mine[w, p] = white[p]
-
-    pair = pltpu.make_async_remote_copy(
-        src_ref=mine.at[pl.ds((1 - core) * half, half)],
-        dst_ref=paired,
-        send_sem=pair_sems.at[0],
-        recv_sem=pair_sems.at[1],
-        device_id={"chan": partner},
-        device_id_type=mesh_id,
-    )
-    pair.start()
-    pair.wait_recv()
-
-    count = line_col.count
-    own = col_buf[0]
-
-    @pl.loop(0, count)
-    def _(k):
-        r, w = k // half, k % half
-        first = (owner_ref[r] == me).astype(f32).astype(bf16)
-        second = (owner_ref[r] == partner).astype(f32).astype(bf16)
-        own[k] = mine[core * half + w] * first + paired[w] * second
+        for j in range(w // half, 2 * cols, 2):
+
+            @pl.when(place != j)
+            def _(j=j, w=w):
+                beside_copy(place, j, w).start()
+
+    for w in range(half):
+        beside[place, w] = mine[core * half + w]
+
+    count = line.count
+    per = count // half
 
     def done_copy(k):
         return pltpu.make_async_remote_copy(
@@ -282,31 +278,40 @@
             device_id_type=mesh_id,
         )
 
-    @pl.loop(0, count + cols + rows - 2)
+    @pl.loop(0, count + LAG * (rows - 1))
     def _(t):
-        k = t - (cols - 1)
-        line_col.tick(t)
-
-        @pl.when(jnp.logical_and(k >= 0, k < count))
+        @pl.when(t < count)
         def _():
-            line_row.own[k] = line_col.result(k)
-
-        line_row.tick(t)
-        last = t - (cols - 1) - (rows - 1)
-
-        @pl.when(jnp.logical_and(last >= 0, last < count))
+            w = t // per
+
+            @pl.when(t % per == 0)
+            def _():
+                for j in range(2 * cols):
+
+                    @pl.when(place != j)
+                    def _(j=j):
+                        beside_copy(j, j, w).wait_recv()
+
+            r, p = (t % per) // 2, t % 2
+            total = jnp.zeros((chans, bins), bf16)
+            for j in range(2 * cols):
+                total += beside[j, w, p] * (owner_ref[r] == base + j).astype(f32).astype(bf16)
+            line.own[t] = total
+
+        line.tick(t)
+        k = t - LAG * (rows - 1)
+
+        @pl.when(k >= 0)
         def _():
-            total = line_row.result(last)
-            done[last] = total
-            done_copy(last).start()
-            for p in range(2):
-                src_ref[last // half, p, core * half + last % half] = total[p]
+            total = line.result(k)
+            done[k] = total
+            done_copy(k).start()
+            src_ref[(k % per) // 2, k % 2, core * half + k // per] = total
 
     @pl.loop(0, count)
     def _(k):
         done_copy(k).wait_recv()
-        for p in range(2):
-            src_ref[k // half, p, (1 - core) * half + k % half] = other[k, p]
+        src_ref[(k % per) // 2, k % 2, (1 - core) * half + k // per] = other[k]
 
     for way in range(2):
         for w in range(wins):
@@ -315,9 +320,14 @@
             def _(way=way, w=w):
                 halo_copy(way, w).wait_send()
 
-    pair.wait_send()
-    line_col.drain()
-    line_row.drain()
+    for w in range(wins):
+        for j in range(w // half, 2 * cols, 2):
+
+            @pl.when(place != j)
+            def _(j=j, w=w):
+                beside_copy(place, j, w).wait_send()
+
+    line.drain()
 
     @pl.loop(0, count)
     def _(k):
@@ -330,9 +340,9 @@
     rounds = owner.shape[0]
     rows, cols = grid
     half = wins // 2
-    count = rounds * half
+    count = rounds * half * 2
     vmem = pl.BlockSpec(memory_space=pltpu.VMEM)
-    chunk = (2, chans, bins)
+    chunk = (chans, bins)
     chunks = pltpu.VMEM((count, *chunk), bf16)
     return pl.pallas_call(
         functools.partial(front_kernel, rows, cols),
@@ -348,15 +358,13 @@
             pltpu.VMEM((bins, bins), bf16),
             pltpu.VMEM((2, wins * chans, bins), f32),
             pltpu.VMEM((2, wins * chans, bins), bf16),
-            pltpu.VMEM((wins, *chunk), bf16),
-            pltpu.VMEM((half, *chunk), bf16),
-            [chunks] * 5,
+            pltpu.VMEM((wins, 2, *chunk), bf16),
+            pltpu.VMEM((2 * cols, half, 2, *chunk), bf16),
             [chunks] * 5,
             chunks,
             chunks,
             pltpu.SemaphoreType.DMA((2, 2, wins)),
-            pltpu.SemaphoreType.DMA((2,)),
-            pltpu.SemaphoreType.DMA((2, 2, count)),
+            pltpu.SemaphoreType.DMA((2, 2 * cols, half)),
             pltpu.SemaphoreType.DMA((2, 2, count)),
             pltpu.SemaphoreType.DMA((2, count)),
         ],

time: 63.4 us -> 50.8 us (0.80)
  Pallas kernels: 62.9 us -> 50.6 us
    pallas_call x1, Pallas kernels: 52.1 us -> 39.8 us  [front(): pl.pallas_call(functools.partial(front_kernel, rows, cols), out_shape=[ja...]
where the time goes in v2:
time: 50.8 us; the launch traced here: 50.6 us
  Pallas kernels  50.6 us (100%)
    pallas_call x1, Pallas kernels, front(): pl.pallas_call(functools.partial(front_kernel, rows, cols), out_shape=[ja...  39.8 us
    pallas_call x1, Pallas kernels, cross(): pl.pallas_call(cross_kernel, out_shape=jax.ShapeDtypeStruct((2, rounds *...  10.7 us

profile of v2, /device:TPU:1, one launch (start us, length us, event | category | flops | bytes accessed | tf_op | source)
XLA Modules:
  0.0 50.6 jit_solution(12205780103600031566)
XLA Ops:
  0.0 39.8 %front.1 = (bf16[2,4,32,512]{3,2,1,0:T(8,128)(2,1)}, bf16[4,2,4,32,512]{4,3,2,1,0:T(8,128)(2,1)}) custom-call(s32[4]{0:T(128)} %owner_ref.1, bf16[2,4,32,512]{3,2,1,0:T(8,128)(2,1)} %own_ref.1, f32[2,8,65]{2,1,0:T(8,128)} %bank_ref.1, s32[1,512]{1,0:T(1,128)} %bitcast.1, s32[4,32]{1,0:T(4,128)} %mask_ref.1), custom_call_target="tpu_custom_call" | custom-call | tf_op jit(solution)/shard_map/front/pallas_call | solution.py:347
  39.8 10.7 %cross.1 = bf16[2,128,32,512]{3,2,1,0:T(8,128)(2,1)} custom-call(s32[4,32]{1,0:T(4,128)} %offset_ref.1, bf16[4,2,4,32,512]{4,3,2,1,0:T(8,128)(2,1)} %get-tuple-element.7.src_ref, bf16[2,4,32,512]{3,2,1,0:T(8,128)(2,1)} %get-tuple-element.8.loc_ref), custom_call_target="tpu_custom_call" | custom-call | tf_op jit(solution)/shard_map/cross/pallas_call | solution.py:423

commit v3 on v2

--- a/solution.py
+++ b/solution.py
@@ -160,16 +160,16 @@
     beside,
     row_buf,
     done,
-    other,
+    gathered,
     halo_sems,
     beside_sems,
     row_sems,
-    done_sems,
+    gather_sems,
 ):
     wins, chans = mask_ref.shape
     bins = own_ref.shape[3]
-    half = wins // 2
-    rounds = src_ref.shape[0]
+    parts = 2 * cols
+    subs, piece = beside.shape[1], beside.shape[2]
     me = lax.axis_index("chan")
     size = rows * cols * 2
     core = me % 2
@@ -206,7 +206,7 @@
             device_id_type=mesh_id,
         )
 
-    order = [c * half + w for w in range(half) for c in range(2)]
+    order = list(range(wins))
     sends = (me < size - 1, me > 0)
     for w in order:
         for way in range(2):
@@ -226,12 +226,12 @@
     build_toeplitz(bank_ref, toep)
     build_window(band)
 
-    def beside_copy(sender, j, w):
+    def beside_copy(sender, j):
         return pltpu.make_async_remote_copy(
-            src_ref=mine.at[w],
-            dst_ref=beside.at[sender, w % half],
-            send_sem=beside_sems.at[0, j, w % half],
-            recv_sem=beside_sems.at[1, sender, w % half],
+            src_ref=mine.at[pl.ds(j * subs, subs)],
+            dst_ref=beside.at[sender],
+            send_sem=beside_sems.at[0, j],
+            recv_sem=beside_sems.at[1, sender],
             device_id={"chan": base + j},
             device_id_type=mesh_id,
         )
@@ -245,73 +245,94 @@
                 halo_copy(way, w).wait_recv()
 
         def x(cut, w=w):
-            parts = []
+            stack = []
             for p in range(2):
-                parts += [halo[0, p, w, :, cut], own_ref[p, w, :, cut], halo[1, p, w, :, cut]]
-                parts += [blank[:, cut]]
-            return jnp.concatenate(parts, axis=0)
+                stack += [halo[0, p, w, :, cut], own_ref[p, w, :, cut], halo[1, p, w, :, cut]]
+                stack += [blank[:, cut]]
+            return jnp.concatenate(stack, axis=0)
 
         filter_window(bank_ref.shape[1], w, x, toep, index_ref, filt, power)
         white = whiten_window(w, band, mask_ref, filt, power)
         for p in range(2):
             out_ref[p, w] = white[p]
-            mine[w, p] = white[p]
-        for j in range(w // half, 2 * cols, 2):
+            for i in range(chans // piece):
+                mine[(w * 2 + p) * (chans // piece) + i] = white[p][i * piece : (i + 1) * piece]
+        for j in range(w * parts // wins, (w + 1) * parts // wins):
 
             @pl.when(place != j)
-            def _(j=j, w=w):
-                beside_copy(place, j, w).start()
-
-    for w in range(half):
-        beside[place, w] = mine[core * half + w]
+            def _(j=j):
+                beside_copy(place, j).start()
+
+    beside[place] = mine[pl.ds(place * subs, subs)]
+    for j in range(parts):
+
+        @pl.when(place != j)
+        def _(j=j):
+            beside_copy(j, j).wait_recv()
 
     count = line.count
-    per = count // half
-
-    def done_copy(k):
+
+    @pl.loop(0, count)
+    def _(k):
+        total = jnp.zeros((piece, bins), bf16)
+        for j in range(parts):
+            total += beside[j, k % subs] * (owner_ref[k // subs] == base + j).astype(f32).astype(bf16)
+        line.own[k] = total
+
+    def give(src, origin, k, sem, who):
         return pltpu.make_async_remote_copy(
-            src_ref=done.at[k],
-            dst_ref=other.at[k],
-            send_sem=done_sems.at[0, k],
-            recv_sem=done_sems.at[1, k],
-            device_id={"chan": partner},
+            src_ref=src,
+            dst_ref=gathered.at[origin, k],
+            send_sem=gather_sems.at[sem, k],
+            recv_sem=gather_sems.at[2 * parts + origin, k],
+            device_id={"chan": who},
             device_id_type=mesh_id,
         )
 
-    @pl.loop(0, count + LAG * (rows - 1))
+    def put(j, k, value):
+        src_ref[k // subs, j * subs + k % subs] = value
+
+    alike = [jnp.logical_and(place != j, core == j % 2) for j in range(parts)]
+    last = LAG * (rows - 1)
+
+    @pl.loop(0, count + last + LAG)
     def _(t):
-        @pl.when(t < count)
-        def _():
-            w = t // per
-
-            @pl.when(t % per == 0)
-            def _():
-                for j in range(2 * cols):
-
-                    @pl.when(place != j)
-                    def _(j=j):
-                        beside_copy(j, j, w).wait_recv()
-
-            r, p = (t % per) // 2, t % 2
-            total = jnp.zeros((chans, bins), bf16)
-            for j in range(2 * cols):
-                total += beside[j, w, p] * (owner_ref[r] == base + j).astype(f32).astype(bf16)
-            line.own[t] = total
-
         line.tick(t)
-        k = t - LAG * (rows - 1)
-
-        @pl.when(k >= 0)
+        k = t - last
+
+        @pl.when(jnp.logical_and(k >= 0, k < count))
         def _():
             total = line.result(k)
             done[k] = total
-            done_copy(k).start()
-            src_ref[(k % per) // 2, k % 2, core * half + k // per] = total
+            for j in range(parts):
+
+                @pl.when(alike[j])
+                def _(j=j):
+                    give(done.at[k], place, k, j, base + j).start()
+
+            give(done.at[k], place, k, parts + place, partner).start()
+            put(place, k, total)
+
+        q = t - last - LAG
+
+        @pl.when(q >= 0)
+        def _():
+            for j in range(parts):
+
+                @pl.when(alike[j])
+                def _(j=j):
+                    give(done.at[q], j, q, j, partner).wait_recv()
+                    give(gathered.at[j, q], j, q, parts + j, partner).start()
+                    put(j, q, gathered[j, q])
 
     @pl.loop(0, count)
     def _(k):
-        done_copy(k).wait_recv()
-        src_ref[(k % per) // 2, k % 2, (1 - core) * half + k // per] = other[k]
+        for j in range(parts):
+
+            @pl.when(core != j % 2)
+            def _(j=j):
+                give(done.at[k], j, k, j, partner).wait_recv()
+                put(j, k, gathered[j, k])
 
     for way in range(2):
         for w in range(wins):
@@ -320,18 +341,23 @@
             def _(way=way, w=w):
                 halo_copy(way, w).wait_send()
 
-    for w in range(wins):
-        for j in range(w // half, 2 * cols, 2):
-
-            @pl.when(place != j)
-            def _(j=j, w=w):
-                beside_copy(place, j, w).wait_send()
+    for j in range(parts):
+
+        @pl.when(place != j)
+        def _(j=j):
+            beside_copy(place, j).wait_send()
 
     line.drain()
 
     @pl.loop(0, count)
     def _(k):
-        done_copy(k).wait_send()
+        give(done.at[k], place, k, parts + place, partner).wait_send()
+        for j in range(parts):
+
+            @pl.when(alike[j])
+            def _(j=j):
+                give(done.at[k], place, k, j, partner).wait_send()
+                give(gathered.at[j, k], j, k, parts + j, partner).wait_send()
 
 
 def front(grid, owner, own, bank, index, mask):
@@ -339,16 +365,19 @@
     nbank = bank.shape[1]
     rounds = owner.shape[0]
     rows, cols = grid
-    half = wins // 2
-    count = rounds * half * 2
+    parts = 2 * cols
+    total = wins * 2 * chans
+    piece = min(chans, total // parts)
+    subs = total // parts // piece
+    count = rounds * subs
     vmem = pl.BlockSpec(memory_space=pltpu.VMEM)
-    chunk = (chans, bins)
+    chunk = (piece, bins)
     chunks = pltpu.VMEM((count, *chunk), bf16)
     return pl.pallas_call(
         functools.partial(front_kernel, rows, cols),
         out_shape=[
             jax.ShapeDtypeStruct(own.shape, bf16),
-            jax.ShapeDtypeStruct((rounds, *own.shape), bf16),
+            jax.ShapeDtypeStruct((rounds, parts * subs, piece, bins), bf16),
         ],
         in_specs=[pl.BlockSpec(memory_space=pltpu.SMEM)] + [vmem] * 4,
         out_specs=[vmem] * 2,
@@ -358,15 +387,15 @@
             pltpu.VMEM((bins, bins), bf16),
             pltpu.VMEM((2, wins * chans, bins), f32),
             pltpu.VMEM((2, wins * chans, bins), bf16),
-            pltpu.VMEM((wins, 2, *chunk), bf16),
-            pltpu.VMEM((2 * cols, half, 2, *chunk), bf16),
+            pltpu.VMEM((parts * subs, *chunk), bf16),
+            pltpu.VMEM((parts, subs, *chunk), bf16),
             [chunks] * 5,
             chunks,
-            chunks,
+            pltpu.VMEM((parts, count, *chunk), bf16),
             pltpu.SemaphoreType.DMA((2, 2, wins)),
-            pltpu.SemaphoreType.DMA((2, 2 * cols, half)),
+            pltpu.SemaphoreType.DMA((2, parts)),
             pltpu.SemaphoreType.DMA((2, 2, count)),
-            pltpu.SemaphoreType.DMA((2, count)),
+            pltpu.SemaphoreType.DMA((3 * parts, count)),
         ],
         compiler_params=pltpu.CompilerParams(collective_id=0, has_side_effects=True),
         name="front",
@@ -379,22 +408,26 @@
     return terms[0]
 
 
-def cross_kernel(offset_ref, src_ref, loc_ref, out_ref, wide):
+def cross_kernel(offset_ref, src_ref, loc_ref, out_ref, wide, held):
     _, wins, chans, bins = loc_ref.shape
     count = out_ref.shape[1]
     r, h = pl.program_id(0), pl.program_id(1)
+
+    @pl.when(jnp.logical_and(r == 0, h == 0))
+    def _():
+        held[...] = loc_ref[...]
 
     @pl.when(h == 0)
     def _():
         for p in range(2):
             for w in range(wins):
-                wide[:, p * wins + w, :] = src_ref[0, p, w].astype(f32) * (1.0 / wins)
+                wide[:, p * wins + w, :] = src_ref[0, w, p].astype(f32) * (1.0 / wins)
 
     for n in range(bins // LANES):
         cut = slice(n * LANES, (n + 1) * LANES)
-        loc = [[loc_ref[p, w, :, cut] for w in range(wins)] for p in range(2)]
-
-        def one(j, carry, cut=cut, loc=loc):
+
+        def one(j, carry, cut=cut):
+            loc = [[held[p, w, :, cut] for w in range(wins)] for p in range(2)]
             at = offset_ref[r, h * count + j]
             src = [
                 [
@@ -418,7 +451,7 @@
 
 
 def cross(offset, src, loc, blocks=2):
-    rounds, _, wins, chans, bins = src.shape
+    rounds, wins, _, chans, bins = src.shape
     per = chans // blocks
     return pl.pallas_call(
         cross_kernel,
@@ -426,11 +459,14 @@
         grid=(rounds, blocks),
         in_specs=[
             pl.BlockSpec(memory_space=pltpu.SMEM),
-            pl.BlockSpec((1, 2, wins, chans, bins), lambda r, h: (r, 0, 0, 0, 0)),
+            pl.BlockSpec((1, wins, 2, chans, bins), lambda r, h: (r, 0, 0, 0, 0)),
             pl.BlockSpec((2, wins, chans, bins), lambda r, h: (0, 0, 0, 0)),
         ],
         out_specs=pl.BlockSpec((2, per, chans, bins), lambda r, h: (0, r * blocks + h, 0, 0)),
-        scratch_shapes=[pltpu.VMEM((chans, 2 * wins, bins), f32)],
+        scratch_shapes=[
+            pltpu.VMEM((chans, 2 * wins, bins), f32),
+            pltpu.VMEM((2, wins, chans, bins), bf16),
+        ],
         name="cross",
     )(offset, src, loc)
 
@@ -448,6 +484,8 @@
     whitened, sources = front(
         grid, owner_order, spectra, filter_bank, band_index[None, :], window_mask
     )
+    _, wins, chans, bins = spectra.shape
+    sources = sources.reshape(sources.shape[0], wins, 2, chans, bins)
     return cross(source_offset, sources, whitened)
 
 

time: 50.8 us -> 48.6 us (0.957)
  Pallas kernels: 50.6 us -> 48.4 us
    pallas_call x1, Pallas kernels: 39.8 us -> 37.6 us  [front(): pl.pallas_call(functools.partial(front_kernel, rows, cols), out_shape=[ja...]
where the time goes in v3:
time: 48.6 us; the launch traced here: 48.4 us
  Pallas kernels  48.4 us (100%)
    pallas_call x1, Pallas kernels, front(): pl.pallas_call(functools.partial(front_kernel, rows, cols), out_shape=[ja...  37.6 us
    pallas_call x1, Pallas kernels, cross(): pl.pallas_call(cross_kernel, out_shape=jax.ShapeDtypeStruct((2, rounds *...  10.7 us

profile of v3, /device:TPU:1, one launch (start us, length us, event | category | flops | bytes accessed | tf_op | source)
XLA Modules:
  0.0 48.4 jit_solution(18424793305816169805)
XLA Ops:
  0.0 37.6 %front.1 = (bf16[2,4,32,512]{3,2,1,0:T(8,128)(2,1)}, bf16[4,8,32,512]{3,2,1,0:T(8,128)(2,1)}) custom-call(s32[4]{0:T(128)} %owner_ref.1, bf16[2,4,32,512]{3,2,1,0:T(8,128)(2,1)} %own_ref.1, f32[2,8,65]{2,1,0:T(8,128)} %bank_ref.1, s32[1,512]{1,0:T(1,128)} %bitcast.3, s32[4,32]{1,0:T(4,128)} %mask_ref.1), custom_call_target="tpu_custom_call" | custom-call | tf_op jit(solution)/shard_map/front/pallas_call | solution.py:376
  37.6 10.7 %cross.1 = bf16[2,128,32,512]{3,2,1,0:T(8,128)(2,1)} custom-call(s32[4,32]{1,0:T(4,128)} %offset_ref.1, bf16[4,4,2,32,512]{4,3,2,1,0:T(8,128)(2,1)} %bitcast.2, bf16[2,4,32,512]{3,2,1,0:T(8,128)(2,1)} %get-tuple-element.8.loc_ref), custom_call_target="tpu_custom_call" | custom-call | tf_op jit(solution)/shard_map/cross/pallas_call | solution.py:456

commit v4 on v3

--- a/solution.py
+++ b/solution.py
@@ -450,7 +450,7 @@
         lax.fori_loop(0, count, one, 0, unroll=4)
 
 
-def cross(offset, src, loc, blocks=2):
+def cross(offset, src, loc, blocks=1):
     rounds, wins, _, chans, bins = src.shape
     per = chans // blocks
     return pl.pallas_call(

time: 48.6 us -> 47.8 us (0.984)
  Pallas kernels: 48.4 us -> 47.6 us
    pallas_call x1, Pallas kernels: 10.7 us -> 9.99 us  [cross(): pl.pallas_call(cross_kernel, out_shape=jax.ShapeDtypeStruct((2, rounds *...]
where the time goes in v4:
time: 47.8 us; the launch traced here: 47.6 us
  Pallas kernels  47.6 us (100%)
    pallas_call x1, Pallas kernels, front(): pl.pallas_call(functools.partial(front_kernel, rows, cols), out_shape=[ja...  37.6 us
    pallas_call x1, Pallas kernels, cross(): pl.pallas_call(cross_kernel, out_shape=jax.ShapeDtypeStruct((2, rounds *...  9.99 us

profile of v4, /device:TPU:1, one launch (start us, length us, event | category | flops | bytes accessed | tf_op | source)
XLA Modules:
  0.0 47.6 jit_solution(10680898248450791268)
XLA Ops:
  0.0 37.6 %front.1 = (bf16[2,4,32,512]{3,2,1,0:T(8,128)(2,1)}, bf16[4,8,32,512]{3,2,1,0:T(8,128)(2,1)}) custom-call(s32[4]{0:T(128)} %owner_ref.1, bf16[2,4,32,512]{3,2,1,0:T(8,128)(2,1)} %own_ref.1, f32[2,8,65]{2,1,0:T(8,128)} %bank_ref.1, s32[1,512]{1,0:T(1,128)} %bitcast.3, s32[4,32]{1,0:T(4,128)} %mask_ref.1), custom_call_target="tpu_custom_call" | custom-call | tf_op jit(solution)/shard_map/front/pallas_call | solution.py:376
  37.6 10.0 %cross.1 = bf16[2,128,32,512]{3,2,1,0:T(8,128)(2,1)} custom-call(s32[4,32]{1,0:T(4,128)} %offset_ref.1, bf16[4,4,2,32,512]{4,3,2,1,0:T(8,128)(2,1)} %bitcast.2, bf16[2,4,32,512]{3,2,1,0:T(8,128)(2,1)} %get-tuple-element.8.loc_ref), custom_call_target="tpu_custom_call" | custom-call | tf_op jit(solution)/shard_map/cross/pallas_call | solution.py:456
